TPU v7x, 256 devices: a whole 4x4x8 slice. The times are simulated.
256 devices in a mesh: rows: 32 (over z, y), cols: 8 (over x, core).
Axes of the slice: x: 4, y: 4, z: 8, core: 2. Of those that a mesh axis runs over, the one named last changes fastest.
Arguments:
- matrix: float32 [32768, 10, 1024], P('rows', None, 'cols'), may hold values from -6 to 6
Outputs:
- reduced: float32 [32768, 10, 1024], P('rows', None, 'cols')
- top_rows: float32 [256, 10, 1024], P(None, None, 'cols')
All inputs are finite; a program needn't handle non-finite values.
Results may differ from a plain program's by a relative error of at most 0.0001.
Values sent between devices are 32-bit elements; how exact they have to be, the bound alone decides.
No kernel may reach another device: no remote copies, remote signals or barrier semaphores. Data moves between devices by JAX's collectives and lax.ppermute only.
A program may use at most 64 MiB of HBM per device.

v0:
```python
import jax
import jax.numpy as jnp
from jax import lax
from jax.sharding import PartitionSpec as P

PRECISE = lax.Precision.HIGHEST


def spread(block, axis, owner):
    block = jnp.where(lax.axis_index(axis) == owner, block, jnp.zeros_like(block))
    return lax.psum(block, axis)


def product(left, right):
    return jnp.dot(left, right, precision=PRECISE, preferred_element_type=jnp.float32)


def relay_panel(panel_block, root_index):
    return spread(panel_block, "cols", root_index)


def factor(panel, columns):
    gram_block = product(panel.T, panel)
    cross_terms = product(panel.T, columns)
    gram_block, cross_terms = lax.psum((gram_block, cross_terms), "rows")
    triangle = jnp.linalg.cholesky(gram_block)
    weights = jax.scipy.linalg.solve_triangular(triangle, cross_terms, lower=True)
    coefficients = jax.scipy.linalg.solve_triangular(triangle, weights, trans=1, lower=True)
    return (weights, columns - product(panel, coefficients))


def shards(matrix):
    rows_dev, rounds, width = matrix.shape
    columns = matrix.reshape(rows_dev, rounds * width)
    first_panel = relay_panel(columns[:, :width], 0)
    first_rows, columns = factor(first_panel, columns)
    second_panel = relay_panel(columns[:, :width], 1)
    second_rows, columns = factor(second_panel, columns)
    triangle_rows = jnp.concatenate([first_rows, second_rows], axis=0)
    return (
        columns.reshape(rows_dev, rounds, width),
        triangle_rows.reshape(2 * width, rounds, width),
    )


def solution(mesh):
    placed = (P("rows", None, "cols"),)
    return jax.shard_map(
        shards,
        mesh=mesh,
        in_specs=placed,
        out_specs=(P("rows", None, "cols"), P(None, None, "cols")),
        check_vma=False,
    )
```

profile of v0, /device:TPU:2, one launch (start us, length us, event | category | flops | bytes accessed | tf_op | source)
XLA Modules:
  0.0 562.0 jit_solution(4598258446387686267)
XLA Ops:
  7.2 5.9 %copy.10 = f32[1024,10,128]{0,2,1:T(8,128)} copy(f32[1024,10,128]{2,0,1:T(8,128)} %param.6) | data formatting | bytes 10485760 | tf_op args[0]
  13.1 5.9 %copy.14 = f32[1024,1280]{1,0:T(8,128)} copy(f32[1024,1280]{0,1:T(8,128)} %bitcast.45) | data formatting | bytes 10485760 | tf_op jit(solution)/shard_map/reshape | solution.py:34
  19.0 1.9 slice_select_fusion.1
  21.0 66.6 %all-reduce.7.cloned.1.call-done = f32[1024,128]{1,0:T(8,128)} async-done(((f32[1024,128]{1,0:T(8,128)}), f32[1024,128]{1,0:T(8,128)}) %all-reduce.7.cloned.1.call-update) | async-done | bytes 524304 | tf_op jit(solution)/shard_map/psum | solution.py:11
  87.6 8.0 %fusion.13 = f32[128,1280]{1,0:T(8,128)} fusion(f32[1024,128]{1,0:T(8,128)} %all-reduce.7.cloned.1.call-done, f32[1024,1280]{0,1:T(8,128)} %bitcast.46), kind=kOutput, calls=%fused_computation.28 | convolution fusion | flops 2013265920 | bytes 6422528 | tf_op jit(solution)/shard_map/dot_general | solution.py:15
  95.5 1.6 fusion.12
  97.4 150.1 %all-reduce.13.cloned.1.call-done = (f32[128,1280]{1,0:T(8,128)}, f32[128,128]{0,1:T(8,128)}) async-done(((f32[128,1280]{1,0:T(8,128)}, f32[128,128]{0,1:T(8,128)}), (f32[128,1280]{1,0:T(8,128)}, f32[128,128]{0,1:T(8,128)})) %all-reduce.13.cloned.1.call-update) | async-done | bytes 720912 | tf_op jit(solution)/shard_map/psum | solution.py:25
  247.5 0.9 copy.13
  248.5 0.9 fusion.11
  249.3 11.7 %cholesky.44 = f32[128,128]{1,0:T(8,128)S(1)} custom-call(f32[128,128]{1,0:T(8,128)S(1)} %fusion.11), custom_call_target="Cholesky" | custom-call | tf_op jit(solution)/shard_map/jit(cholesky)/cholesky | solution.py:26
  261.7 0.7 fusion
  262.4 9.8 %custom-call.11 = f32[1,128,128]{1,2,0:T(8,128)S(1)} custom-call(f32[1,128,128]{2,1,0:T(8,128)S(1)} %fusion), custom_call_target="InvertDiagBlocksLowerTriangular" | custom-call | tf_op jit(solution)/shard_map/jit(_solve_triangular)/triangular_solve | solution.py:28
  272.2 1.8 fusion.7
  274.0 0.7 fusion.9
  274.7 6.4 %convolution_subtract_fusion.1 = f32[1024,1280]{1,0:T(8,128)S(1)} fusion(f32[1024,1280]{1,0:T(8,128)} %copy.14, f32[1024,128]{1,0:T(8,128)S(1)} %copy-done.1, f32[128,1280]{1,0:T(8,128)S(1)} %fusion.9), kind=kOutput, calls=%fused_computation.1 | convolution fusion | flops 2014576640 | bytes 11665408 | tf_op jit(solution)/shard_map/dot_general | solution.py:15
  281.1 2.3 copy-done
  283.4 0.8 slice_select_fusion
  284.6 60.2 %all-reduce.9.cloned.1.call-done = f32[1024,128]{1,0:T(8,128)} async-done(((f32[1024,128]{1,0:T(8,128)}), f32[1024,128]{1,0:T(8,128)}) %all-reduce.9.cloned.1.call-update) | async-done | bytes 524304 | tf_op jit(solution)/shard_map/psum | solution.py:11
  344.8 2.9 fusion.14
  347.6 6.3 %fusion.15 = f32[128,1280]{1,0:T(8,128)} fusion(f32[1024,128]{1,0:T(8,128)} %all-reduce.9.cloned.1.call-done, f32[1024,1280]{1,0:T(8,128)} %copy-done), kind=kOutput, calls=%fused_computation.30 | convolution fusion | flops 2013265920 | bytes 6422528 | tf_op jit(solution)/shard_map/dot_general | solution.py:15
  354.0 150.2 %all-reduce.11.cloned.1.call-done = (f32[128,1280]{1,0:T(8,128)}, f32[128,128]{0,1:T(8,128)}) async-done(((f32[128,1280]{1,0:T(8,128)}, f32[128,128]{0,1:T(8,128)}), (f32[128,1280]{1,0:T(8,128)}, f32[128,128]{0,1:T(8,128)})) %all-reduce.11.cloned.1.call-update) | async-done | bytes 720912 | tf_op jit(solution)/shard_map/psum | solution.py:25
  504.2 0.9 copy.16
  505.2 0.9 fusion.6
  506.0 11.7 %cholesky.55 = f32[128,128]{1,0:T(8,128)S(1)} custom-call(f32[128,128]{1,0:T(8,128)S(1)} %fusion.6), custom_call_target="Cholesky" | custom-call | tf_op jit(solution)/shard_map/jit(cholesky)/cholesky | solution.py:26
  519.1 9.8 %custom-call.13 = f32[1,128,128]{1,2,0:T(8,128)S(1)} custom-call(f32[1,128,128]{2,1,0:T(8,128)S(1)} %fusion.1), custom_call_target="InvertDiagBlocksLowerTriangular" | custom-call | tf_op jit(solution)/shard_map/jit(_solve_triangular)/triangular_solve | solution.py:28
  528.9 1.8 fusion.2
  530.7 0.7 fusion.4
  531.5 7.9 %convolution_subtract_fusion = f32[1024,1280]{1,0:T(8,128)} fusion(f32[1024,1280]{1,0:T(8,128)} %copy-done, f32[1024,128]{1,0:T(8,128)S(1)} %copy-done.2, f32[128,1280]{1,0:T(8,128)S(1)} %fusion.4), kind=kOutput, calls=%fused_computation | convolution fusion | flops 2014576640 | bytes 11665408 | tf_op jit(solution)/shard_map/dot_general | solution.py:15
  539.4 5.9 %copy.17 = f32[1024,1280]{0,1:T(8,128)} copy(f32[1024,1280]{1,0:T(8,128)} %convolution_subtract_fusion) | data formatting | bytes 10485760 | tf_op jit(solution)/shard_map/sub | solution.py:29
  545.4 5.9 %copy.19 = f32[1024,10,128]{2,0,1:T(8,128)} copy(f32[1024,10,128]{0,2,1:T(8,128)} %bitcast.47) | data formatting | bytes 10485760
  551.2 1.5 copy.18
  552.7 2.8 copy.20
  (19 shorter events, 2.7 us)
Async XLA Ops:
  7.2 80.4 %all-reduce.7.cloned.1.call-start = ((), (), s32[]{:S(2)}) async-start(), calls=%async_computation | async-start | bytes 1048576 | tf_op jit(solution)/shard_map/psum | solution.py:11
  20.9 226.6 %all-reduce.13.cloned.1.call-start = ((), (), s32[]{:S(2)}) async-start(), calls=%async_computation.3 | async-start | bytes 1441792 | tf_op jit(solution)/shard_map/psum | solution.py:25
  87.6 8.0 %copy-start.1 = (f32[1024,128]{1,0:T(8,128)S(1)}, f32[1024,128]{1,0:T(8,128)}, u32[]{:S(2)}) copy-start(f32[1024,128]{1,0:T(8,128)} %all-reduce.7.cloned.1.call-done) | copy-start | bytes 1572868
  97.2 247.6 %all-reduce.9.cloned.1.call-start = ((), (), s32[]{:S(2)}) async-start(), calls=%async_computation.1 | async-start | bytes 1048576 | tf_op jit(solution)/shard_map/psum | solution.py:11
  281.1 2.4 copy-start
  284.3 220.0 %all-reduce.11.cloned.1.call-start = ((), (), s32[]{:S(2)}) async-start(), calls=%async_computation.2 | async-start | bytes 1441792 | tf_op jit(solution)/shard_map/psum | solution.py:25
  347.6 183.9 %copy-start.2 = (f32[1024,128]{1,0:T(8,128)S(1)}, f32[1024,128]{1,0:T(8,128)}, u32[]{:S(2)}) copy-start(f32[1024,128]{1,0:T(8,128)} %all-reduce.9.cloned.1.call-done) | copy-start | bytes 1572868
Sparse Core Ops, SparseCore 0:
  21.1 66.4 all-reduce.6
  97.3 150.1 all-reduce.12
  284.4 60.3 all-reduce.8
  354.1 150.0 all-reduce.10
where the time goes:
time: 563 us; the launch traced here: 562 us
  waiting for transfers between devices  427 us (76%)
  other arithmetic  50.2 us (9%)
  matrix products  38.1 us (7%)
  local copies, waits for them, and re-layouts  32.1 us (6%)
  between operations  13.9 us (2%)
    psum x2, waiting for transfers between devices, factor(): gram_block, cross_terms = lax.psum((gram_block, cross_terms), 'rows')  300 us
    psum x2, waiting for transfers between devices, spread(): return lax.psum(block, axis)  127 us
    dot_general x6, matrix products, product(): jnp.dot(left, right, precision=PRECISE, preferred_element_type=jnp.float32)  33.1 us
    another operation x6, other arithmetic, factor(): triangle = jnp.linalg.cholesky(gram_block)  24.8 us
    another operation x4, other arithmetic, factor(): jax.scipy.linalg.solve_triangular(triangle, weights, trans=1, lower=True)  20.9 us
    unnamed x9, local copies, waits for them, and re-layouts  16.9 us
  transfers between devices with their start and end apart: 4, of which 4 were waited for; matrix products, arithmetic and copies ran while one was open for 0% of the time, Pallas kernels for 0%

commit v1 on v0

--- a/solution.py
+++ b/solution.py
@@ -8,7 +8,7 @@
 
 def spread(block, axis, owner):
     block = jnp.where(lax.axis_index(axis) == owner, block, jnp.zeros_like(block))
-    return lax.psum(block, axis)
+    return jnp.sum(lax.all_gather(block, axis), axis=0)
 
 
 def product(left, right):

time: 563 us -> 506 us (0.90)
  waiting for transfers between devices: 427 us -> 366 us
    psum x2 -> x0, waiting for transfers between devices: 127 us -> none  [spread(): return lax.psum(block, axis)]
    all_gather x0 -> x2, waiting for transfers between devices: none -> 66.9 us  [spread(): return jnp.sum(lax.all_gather(block, axis), axis=0)]
    unnamed x9 -> x5, local copies, waits for them, and re-layouts: 16.9 us -> 16.9 us
where the time goes in v1:
time: 506 us; the launch traced here: 505 us
  waiting for transfers between devices  366 us (72%)
  other arithmetic  55.1 us (11%)
  matrix products  36.4 us (7%)
  local copies, waits for them, and re-layouts  32.1 us (6%)
  between operations  13.9 us (3%)
    psum x2, waiting for transfers between devices, factor(): gram_block, cross_terms = lax.psum((gram_block, cross_terms), 'rows')  299 us
    all_gather x2, waiting for transfers between devices, spread(): return jnp.sum(lax.all_gather(block, axis), axis=0)  66.9 us
    dot_general x6, matrix products, product(): jnp.dot(left, right, precision=PRECISE, preferred_element_type=jnp.float32)  31.5 us
    another operation x6, other arithmetic, factor(): triangle = jnp.linalg.cholesky(gram_block)  24.8 us
    another operation x4, other arithmetic, factor(): jax.scipy.linalg.solve_triangular(triangle, weights, trans=1, lower=True)  20.9 us
    unnamed x5, local copies, waits for them, and re-layouts  16.9 us
  transfers between devices with their start and end apart: 4, of which 4 were waited for; matrix products, arithmetic and copies ran while one was open for 0% of the time, Pallas kernels for 0%

profile of v1, /device:TPU:2, one launch (start us, length us, event | category | flops | bytes accessed | tf_op | source)
XLA Modules:
  0.0 504.5 jit_solution(17908171459436652079)
XLA Ops:
  7.2 5.9 %copy.10 = f32[1024,10,128]{0,2,1:T(8,128)} copy(f32[1024,10,128]{2,0,1:T(8,128)} %param.6) | data formatting | bytes 10485760 | tf_op args[0]
  13.1 5.9 %copy.14 = f32[1024,1280]{1,0:T(8,128)} copy(f32[1024,1280]{0,1:T(8,128)} %bitcast.47) | data formatting | bytes 10485760 | tf_op jit(solution)/shard_map/reshape | solution.py:34
  19.0 1.9 slice_select_fusion.1
  21.0 36.7 %all-gather.5.cloned.1.call-done = f32[8192,128]{1,0:T(8,128)} async-done(((f32[1024,128]{1,0:T(8,128)}), f32[8192,128]{1,0:T(8,128)}) %all-gather.5.cloned.1.call-update) | async-done | bytes 4194320 | tf_op jit(solution)/shard_map/all_gather | solution.py:11
  57.7 2.4 reduce_sum.18
  60.1 7.8 %fusion.13 = f32[128,1280]{1,0:T(8,128)} fusion(f32[1024,128]{1,0:T(8,128)S(1)} %reduce_sum.18, f32[1024,1280]{0,1:T(8,128)} %bitcast.48), kind=kOutput, calls=%fused_computation.28 | convolution fusion | flops 2013265920 | bytes 6422528 | tf_op jit(solution)/shard_map/dot_general | solution.py:15
  67.9 1.6 fusion.12
  69.8 149.7 %all-reduce.7.cloned.1.call-done = (f32[128,1280]{1,0:T(8,128)}, f32[128,128]{0,1:T(8,128)}) async-done(((f32[128,1280]{1,0:T(8,128)}, f32[128,128]{0,1:T(8,128)}), (f32[128,1280]{1,0:T(8,128)}, f32[128,128]{0,1:T(8,128)})) %all-reduce.7.cloned.1.call-update) | async-done | bytes 720912 | tf_op jit(solution)/shard_map/psum | solution.py:25
  219.4 0.9 copy.13
  220.4 0.9 fusion.11
  221.2 11.7 %cholesky.44 = f32[128,128]{1,0:T(8,128)S(1)} custom-call(f32[128,128]{1,0:T(8,128)S(1)} %fusion.11), custom_call_target="Cholesky" | custom-call | tf_op jit(solution)/shard_map/jit(cholesky)/cholesky | solution.py:26
  234.3 9.8 %custom-call.11 = f32[1,128,128]{1,2,0:T(8,128)S(1)} custom-call(f32[1,128,128]{2,1,0:T(8,128)S(1)} %fusion), custom_call_target="InvertDiagBlocksLowerTriangular" | custom-call | tf_op jit(solution)/shard_map/jit(_solve_triangular)/triangular_solve | solution.py:28
  244.1 1.8 fusion.7
  245.9 0.7 fusion.9
  246.6 6.4 %convolution_subtract_fusion.1 = f32[1024,1280]{1,0:T(8,128)S(1)} fusion(f32[1024,1280]{1,0:T(8,128)} %copy.14, f32[1024,128]{1,0:T(8,128)S(1)} %reduce_sum.18, f32[128,1280]{1,0:T(8,128)S(1)} %fusion.9), kind=kOutput, calls=%fused_computation.1 | convolution fusion | flops 2014576640 | bytes 11665408 | tf_op jit(solution)/shard_map/dot_general | solution.py:15
  253.0 2.3 copy-done
  255.4 0.8 slice_select_fusion
  256.5 30.2 %all-gather.7.cloned.1.call-done = f32[8192,128]{1,0:T(8,128)} async-done(((f32[1024,128]{1,0:T(8,128)}), f32[8192,128]{1,0:T(8,128)}) %all-gather.7.cloned.1.call-update) | async-done | bytes 4194320 | tf_op jit(solution)/shard_map/all_gather | solution.py:11
  286.7 2.4 reduce_sum.19
  289.2 1.6 fusion.14
  290.8 6.1 %fusion.15 = f32[128,1280]{1,0:T(8,128)} fusion(f32[1024,128]{1,0:T(8,128)S(1)} %reduce_sum.19, f32[1024,1280]{1,0:T(8,128)} %copy-done), kind=kOutput, calls=%fused_computation.30 | convolution fusion | flops 2013265920 | bytes 6422528 | tf_op jit(solution)/shard_map/dot_general | solution.py:15
  296.9 149.8 %all-reduce.5.cloned.1.call-done = (f32[128,1280]{1,0:T(8,128)}, f32[128,128]{0,1:T(8,128)}) async-done(((f32[128,1280]{1,0:T(8,128)}, f32[128,128]{0,1:T(8,128)}), (f32[128,1280]{1,0:T(8,128)}, f32[128,128]{0,1:T(8,128)})) %all-reduce.5.cloned.1.call-update) | async-done | bytes 720912 | tf_op jit(solution)/shard_map/psum | solution.py:25
  446.7 0.9 copy.16
  447.7 0.9 fusion.6
  448.5 11.7 %cholesky.55 = f32[128,128]{1,0:T(8,128)S(1)} custom-call(f32[128,128]{1,0:T(8,128)S(1)} %fusion.6), custom_call_target="Cholesky" | custom-call | tf_op jit(solution)/shard_map/jit(cholesky)/cholesky | solution.py:26
  461.6 9.8 %custom-call.13 = f32[1,128,128]{1,2,0:T(8,128)S(1)} custom-call(f32[1,128,128]{2,1,0:T(8,128)S(1)} %fusion.1), custom_call_target="InvertDiagBlocksLowerTriangular" | custom-call | tf_op jit(solution)/shard_map/jit(_solve_triangular)/triangular_solve | solution.py:28
  471.4 1.8 fusion.2
  474.0 7.9 %convolution_subtract_fusion = f32[1024,1280]{1,0:T(8,128)} fusion(f32[1024,1280]{1,0:T(8,128)} %copy-done, f32[1024,128]{1,0:T(8,128)S(1)} %reduce_sum.19, f32[128,1280]{1,0:T(8,128)S(1)} %fusion.4), kind=kOutput, calls=%fused_computation | convolution fusion | flops 2014576640 | bytes 11665408 | tf_op jit(solution)/shard_map/dot_general | solution.py:15
  481.9 5.9 %copy.17 = f32[1024,1280]{0,1:T(8,128)} copy(f32[1024,1280]{1,0:T(8,128)} %convolution_subtract_fusion) | data formatting | bytes 10485760 | tf_op jit(solution)/shard_map/sub | solution.py:29
  487.9 5.9 %copy.19 = f32[1024,10,128]{2,0,1:T(8,128)} copy(f32[1024,10,128]{0,2,1:T(8,128)} %bitcast.49) | data formatting | bytes 10485760
  493.7 1.5 copy.18
  495.2 2.8 copy.20
  (17 shorter events, 4.1 us)
Async XLA Ops:
  7.2 50.5 %all-gather.5.cloned.1.call-start = ((), (), s32[]{:S(2)}) async-start(), calls=%async_computation | async-start | bytes 4718592 | tf_op jit(solution)/shard_map/all_gather | solution.py:11
  20.9 198.5 %all-reduce.7.cloned.1.call-start = ((), (), s32[]{:S(2)}) async-start(), calls=%async_computation.3 | async-start | bytes 1441792 | tf_op jit(solution)/shard_map/psum | solution.py:25
  69.5 217.2 %all-gather.7.cloned.1.call-start = ((), (), s32[]{:S(2)}) async-start(), calls=%async_computation.1 | async-start | bytes 4718592 | tf_op jit(solution)/shard_map/all_gather | solution.py:11
  253.0 2.4 copy-start
  256.2 190.5 %all-reduce.5.cloned.1.call-start = ((), (), s32[]{:S(2)}) async-start(), calls=%async_computation.2 | async-start | bytes 1441792 | tf_op jit(solution)/shard_map/psum | solution.py:25
Sparse Core Ops, SparseCore 0:
  21.1 36.5 all-gather.4
  69.7 149.7 all-reduce.6
  256.3 30.3 all-gather.6
  297.1 149.6 all-reduce.4
